TPU v7x, 128 devices: a whole 4x4x4 slice. The times are simulated.
128 devices in a mesh: dp: 32 (over y, z, core), expert: 4 (over x).
Axes of the slice: x: 4, y: 4, z: 4, core: 2. Of those that a mesh axis runs over, the one named last changes fastest.
Arguments:
- grad_parts: bfloat16 [32, 2048, 6144], P('dp', 'expert')
- bucket_order: int32 [256], replicated, may hold values from 0 to 255, each once
- master: float32 [4, 32, 16, 6144], P('expert', 'dp'), may hold values from -6 to 6
- first_moment: float32 [4, 32, 16, 6144], P('expert', 'dp'), may hold values from -0.6 to 0.6
- second_moment: float32 [4, 32, 16, 6144], P('expert', 'dp'), may hold values from 0.01 to 1
- step_count: int32 [4, 32, 16], P('expert', 'dp'), may hold values from 1 to 8
- max_rms: float32 [1], replicated, may hold values from 0.3 to 1
Outputs:
- new_master: float32 [4, 32, 16, 6144], P('expert', 'dp')
- new_first: float32 [4, 32, 16, 6144], P('expert', 'dp')
- new_second: float32 [4, 32, 16, 6144], P('expert', 'dp')
- new_params: bfloat16 [2048, 6144], P('expert')
Inputs may be any that keep to these rules, and one draw needn't show every extreme that they name: bucket_order is a permutation of the 256 buckets.
All inputs are finite; a program needn't handle non-finite values.
Results may differ from a plain program's by a relative error of at most 0.0085.
Values may be sent and summed in bfloat16 or wider, within the bound.
A program may use at most 128 MiB of HBM per device.

v0:
```python
import jax
import jax.numpy as jnp
from jax import lax
from jax.sharding import Mesh
from jax.sharding import PartitionSpec as P

DP = ("dp_0", "dp_1", "dp_2")
DP_EXPERT = ("dp_0", "dp_1", "dp_2", "expert")


def by_axis(shard, axes):
    for axis in axes:
        shard = lax.psum(shard, axis)
    return shard


def shards(grad_parts, bucket_order, master, first_moment, second_moment, step_count, max_rms):
    dp_count = lax.axis_size(DP)
    local_grad = grad_parts[0]
    rows_dev, row_width = local_grad.shape
    bucket_count = bucket_order.shape[0]
    bucket_rows = rows_dev // bucket_count
    owner_rows = rows_dev // dp_count
    buckets = local_grad.reshape(bucket_count, bucket_rows, row_width)
    slotted = jnp.take(buckets, bucket_order, axis=0)
    pieces = slotted.reshape(dp_count, owner_rows, row_width)
    received = lax.all_to_all(pieces, DP, split_axis=0, concat_axis=0, tiled=True)
    owned_sum = jnp.sum(received.astype(jnp.float32), axis=0)
    square_sum = by_axis(jnp.sum(owned_sum * owned_sum), DP_EXPERT)
    entries = float(rows_dev * row_width * lax.axis_size("expert"))
    clip_factor = jnp.minimum(1.0, max_rms[0] / jnp.sqrt(square_sum / entries + 1e-06))
    clipped = clip_factor * owned_sum
    new_first = 0.9 * first_moment[0, 0] + 0.1 * clipped
    new_second = 0.95 * second_moment[0, 0] + 0.05 * clipped * clipped
    step_float = step_count[0, 0].astype(jnp.float32)[:, None]
    first_fix = 1.0 - jnp.power(jnp.float32(0.9), step_float)
    second_fix = 1.0 - jnp.power(jnp.float32(0.95), step_float)
    ratio = new_first / first_fix / (jnp.sqrt(new_second / second_fix) + 1e-08)
    old_master = master[0, 0]
    new_master = old_master - 0.1 * (ratio + 0.1 * old_master)
    fresh = new_master.astype(jnp.bfloat16)
    gathered = lax.all_gather(fresh, DP, axis=0, tiled=True)
    slot_rows = gathered.reshape(bucket_count, bucket_rows, row_width)
    placed = jnp.zeros_like(slot_rows).at[bucket_order].set(slot_rows)
    return (
        new_master[None, None],
        new_first[None, None],
        new_second[None, None],
        placed.reshape(rows_dev, row_width),
    )


def solution(mesh):
    finer = Mesh(
        mesh.devices.reshape(4, 4, 2, mesh.shape["expert"]), ("dp_0", "dp_1", "dp_2", "expert")
    )
    return jax.shard_map(
        shards,
        mesh=finer,
        in_specs=(
            P(DP, "expert", None),
            P(),
            P("expert", DP, None, None),
            P("expert", DP, None, None),
            P("expert", DP, None, None),
            P("expert", DP, None),
            P(),
        ),
        out_specs=(
            P("expert", DP, None, None),
            P("expert", DP, None, None),
            P("expert", DP, None, None),
            P("expert", None),
        ),
        check_vma=False,
    )
```

profile of v0, /device:TPU:1, one launch (start us, length us, event | category | flops | bytes accessed | tf_op | source)
XLA Modules:
  0.0 324.7 jit_solution(6990627226799949666)
XLA Ops:
  7.2 0.0 all-gather.2.cloned.1.call-start
  7.2 0.7 compare_and_fusion
  7.9 0.7 compare_select_fusion
  8.6 0.1 broadcast_in_dim.26
  8.7 0.1 copy.11
  8.8 0.1 copy.12
  8.9 12.8 %reshape_squeeze.3 = bf16[256,2,6144]{2,1,0:T(2,128)(2,1)} reshape(bf16[1,512,6144]{2,1,0:T(8,128)(2,1)} %param.7) | data formatting | bytes 12582912 | tf_op jit(solution)/shard_map/reshape;squeeze | solution.py:24
  21.7 21.4 %gather_fusion = bf16[256,2,6144]{2,1,0:T(2,128)(2,1)} fusion(bf16[256,2,6144]{2,1,0:T(2,128)(2,1)} %reshape_squeeze.3, s32[1024]{0:T(1024)S(1)} %pad_clamp_fusion), kind=kCustom, calls=%fused_computation | custom fusion | bytes 12583936 | tf_op jit(solution)/shard_map/jit(_take)/gather | solution.py:25
  43.1 13.3 %gather.7 = bf16[32,16,6144]{2,1,0:T(8,128)(2,1)} reshape(bf16[256,2,6144]{2,1,0:T(2,128)(2,1)} %gather_fusion) | data formatting | bytes 12582912 | tf_op jit(solution)/shard_map/jit(_take)/gather | solution.py:25
  56.4 3.4 %broadcast_select_fusion = bf16[32,16,6144]{2,1,0:T(8,128)(2,1)S(1)} fusion(bf16[32,16,6144]{2,1,0:T(8,128)(2,1)} %gather.7, pred[32,16]{1,0:T(8,128)(4,1)S(1)} %copy.12), kind=kLoop, calls=%fused_computation.3 | loop fusion | flops 3145728 | bytes 12583424 | tf_op jit(solution)/shard_map/jit(_take)/select_n | solution.py:25
  59.9 82.5 %all_to_all.5 = bf16[32,16,6144]{2,1,0:T(8,128)(2,1)S(1)} all-to-all(bf16[32,16,6144]{2,1,0:T(8,128)(2,1)S(1)} %broadcast_select_fusion), channel_id=1, replica_groups=mesh['dp_0'=4,'dp_1'=4,'dp_2'=2,'expert'=4] {'dp_0','dp_1','dp_2'}, dimensions={0} | all-to-all | bytes 12582912 | tf_op jit(solution)/shard_map/all_to_all | solution.py:27
  142.4 0.0 copy-start.3
  142.4 0.0 copy-start
  142.4 0.0 copy-start.1
  142.4 0.0 copy-start.2
  142.4 1.0 convert_reduce_fusion
  143.4 0.7 multiply_reduce_fusion
  144.1 7.3 %psum.28 = f32[]{:T(128)} all-reduce(f32[]{:T(128)} %multiply_reduce_fusion), channel_id=1, replica_groups=mesh['dp_0'=4,'dp_1'=4,'dp_2'=2,'expert'=4] {'dp_0'}, use_global_device_ids=true, to_apply=%region_2.3 | all-reduce | flops 1 | bytes 8 | tf_op jit(solution)/shard_map/psum | solution.py:13
  151.5 8.0 %psum.29 = f32[]{:T(128)} all-reduce(f32[]{:T(128)} %psum.28), channel_id=1, replica_groups=mesh['dp_0'=4,'dp_1'=4,'dp_2'=2,'expert'=4] {'dp_1'}, use_global_device_ids=true, to_apply=%region_3.4 | all-reduce | flops 1 | bytes 8 | tf_op jit(solution)/shard_map/psum | solution.py:13
  159.4 0.0 copy-done.3
  159.4 7.0 %psum.30 = f32[]{:T(128)} all-reduce(f32[]{:T(128)} %psum.29), channel_id=1, replica_groups=mesh['dp_0'=4,'dp_1'=4,'dp_2'=2,'expert'=4] {'dp_2'}, use_global_device_ids=true, to_apply=%region_4.5 | all-reduce | flops 1 | bytes 8 | tf_op jit(solution)/shard_map/psum | solution.py:13
  167.0 9.3 %psum.31 = f32[]{:T(128)} all-reduce(f32[]{:T(128)} %psum.30), channel_id=1, replica_groups=mesh['dp_0'=4,'dp_1'=4,'dp_2'=2,'expert'=4] {'expert'}, use_global_device_ids=true, to_apply=%region_5.6 | all-reduce | flops 1 | bytes 8 | tf_op jit(solution)/shard_map/psum | solution.py:13
  177.0 0.0 copy-done
  177.0 0.0 copy-done.1
  177.0 0.0 copy-done.2
  177.1 1.0 fusion.9
  178.1 0.0 all-gather.2.cloned.1.call-update
  178.1 1.2 multiply_subtract_fusion
  179.3 45.1 %all-gather.2.cloned.1.call-done = bf16[512,6144]{1,0:T(8,128)(2,1)} async-done(((bf16[16,6144]{1,0:T(8,128)(2,1)}), bf16[512,6144]{1,0:T(8,128)(2,1)}) %all-gather.2.cloned.1.call-update) | async-done | bytes 6291472 | tf_op jit(solution)/shard_map/all_gather | solution.py:42
  224.4 12.8 %reshape.105 = bf16[256,2,6144]{2,1,0:T(2,128)(2,1)} reshape(bf16[512,6144]{1,0:T(8,128)(2,1)} %all-gather.2.cloned.1.call-done) | data formatting | bytes 12582912 | tf_op jit(solution)/shard_map/reshape | solution.py:43
  237.2 5.9 %broadcast_in_dim.32 = bf16[256,2,6144]{2,1,0:T(2,128)(2,1)} broadcast(bf16[]{:T(256)} %constant.13.clone.1), dimensions={} | broadcast | bytes 6291458 | tf_op jit(solution)/shard_map/broadcast_in_dim | solution.py:44
  243.1 61.5 %scatter_fusion = bf16[256,2,6144]{2,1,0:T(2,128)(2,1)} fusion(bf16[256,2,6144]{2,1,0:T(2,128)(2,1)} %broadcast_in_dim.32, s32[256]{0:T(256)S(1)} %compare_select_fusion, bf16[256,2,6144]{2,1,0:T(2,128)(2,1)} %reshape.105), kind=kCustom, calls=%fused_computation.1 | custom fusion | bytes 18875392 | tf_op jit(solution)/shard_map/scatter | solution.py:44
  304.6 13.3 %reshape.92 = bf16[512,6144]{1,0:T(8,128)(2,1)} reshape(bf16[256,2,6144]{2,1,0:T(2,128)(2,1)} %scatter_fusion) | data formatting | bytes 12582912 | tf_op jit(solution)/shard_map/reshape | solution.py:49
  (4 shorter events, 0.0 us)
Async XLA Ops:
  7.2 217.2 %all-gather.2.cloned.1.call-start = ((), (), s32[]{:S(2)}) async-start(), calls=%async_computation.1 | async-start | bytes 6488064 | tf_op jit(solution)/shard_map/all_gather | solution.py:42
  142.4 17.0 %copy-start.3 = (s32[1,1,16]{2,1,0:T(1,128)S(1)}, s32[1,1,16]{2,1,0:T(1,128)}, u32[]{:S(2)}) copy-start(s32[1,1,16]{2,1,0:T(1,128)} %param.12) | copy-start | bytes 196
  142.4 34.6 %copy-start = (f32[1,1,16,6144]{3,2,1,0:T(8,128)S(1)}, f32[1,1,16,6144]{3,2,1,0:T(8,128)}, u32[]{:S(2)}) copy-start(f32[1,1,16,6144]{3,2,1,0:T(8,128)} %param.9) | copy-start | bytes 1179652
  142.4 34.7 %copy-start.1 = (f32[1,1,16,6144]{3,2,1,0:T(8,128)S(1)}, f32[1,1,16,6144]{3,2,1,0:T(8,128)}, u32[]{:S(2)}) copy-start(f32[1,1,16,6144]{3,2,1,0:T(8,128)} %param.11) | copy-start | bytes 1179652
  142.4 34.7 %copy-start.2 = (f32[1,1,16,6144]{3,2,1,0:T(8,128)S(1)}, f32[1,1,16,6144]{3,2,1,0:T(8,128)}, u32[]{:S(2)}) copy-start(f32[1,1,16,6144]{3,2,1,0:T(8,128)} %param.10) | copy-start | bytes 1179652
Sparse Core Ops, SparseCore 0:
  178.2 46.1 all-gather.1
where the time goes:
time: 327 us; the launch traced here: 325 us
  local copies, waits for them, and re-layouts  141 us (43%)
  blocking collectives  114 us (35%)
  waiting for transfers between devices  45.1 us (14%)
  between operations  15.4 us (5%)
  other arithmetic  8.79 us (3%)
    all_to_all x1, blocking collectives, shards(): lax.all_to_all(pieces, DP, split_axis=0, concat_axis=0, tiled=True)  82.5 us
    scatter x1, local copies, waits for them, and re-layouts, shards(): placed = jnp.zeros_like(slot_rows).at[bucket_order].set(slot_rows)  61.5 us
    all_gather x1, waiting for transfers between devices, shards(): gathered = lax.all_gather(fresh, DP, axis=0, tiled=True)  45.1 us
    gather x2, local copies, waits for them, and re-layouts, shards(): slotted = jnp.take(buckets, bucket_order, axis=0)  34.7 us
    psum x4, blocking collectives, by_axis(): shard = lax.psum(shard, axis)  31.5 us
    reshape x1, local copies, waits for them, and re-layouts, shards(): placed.reshape(rows_dev, row_width)  13.3 us
    another operation x1, local copies, waits for them, and re-layouts, shards(): buckets = local_grad.reshape(bucket_count, bucket_rows, row_width)  12.8 us
    reshape x1, local copies, waits for them, and re-layouts, shards(): slot_rows = gathered.reshape(bucket_count, bucket_rows, row_width)  12.8 us
  transfers between devices with their start and end apart: 1, of which 1 were waited for; matrix products, arithmetic and copies ran while one was open for 0% of the time, Pallas kernels for 0%

commit v1 on v0

--- a/solution.py
+++ b/solution.py
@@ -39,7 +39,9 @@
     old_master = master[0, 0]
     new_master = old_master - 0.1 * (ratio + 0.1 * old_master)
     fresh = new_master.astype(jnp.bfloat16)
-    gathered = lax.all_gather(fresh, DP, axis=0, tiled=True)
+    gathered = jnp.concatenate(
+        lax.all_to_all(jnp.stack([fresh] * lax.axis_size(DP)), DP, 0, 0), axis=0
+    )
     slot_rows = gathered.reshape(bucket_count, bucket_rows, row_width)
     placed = jnp.zeros_like(slot_rows).at[bucket_order].set(slot_rows)
     return (

time: 327 us -> 363 us (1.11)
  the two profiles are of different devices: /device:TPU:1 before, /device:TPU:32 now
where the time goes in v1:
time: 363 us; the launch traced here: 361 us
  local copies, waits for them, and re-layouts  145 us (40%)
  blocking collectives  114 us (31%)
  waiting for transfers between devices  86.5 us (24%)
  other arithmetic  8.12 us (2%)
  starting transfers between devices  5.67 us (2%)
    all_to_all x1, waiting for transfers between devices, shards(): lax.all_to_all(jnp.stack([fresh] * lax.axis_size(DP)), DP, 0, 0)  86.5 us
    all_to_all x1, blocking collectives, shards(): lax.all_to_all(pieces, DP, split_axis=0, concat_axis=0, tiled=True)  79.7 us
    scatter x1, local copies, waits for them, and re-layouts, shards(): placed = jnp.zeros_like(slot_rows).at[bucket_order].set(slot_rows)  61.5 us
    gather x2, local copies, waits for them, and re-layouts, shards(): slotted = jnp.take(buckets, bucket_order, axis=0)  34.7 us
    psum x4, blocking collectives, by_axis(): shard = lax.psum(shard, axis)  33.9 us
    reshape x1, local copies, waits for them, and re-layouts, shards(): placed.reshape(rows_dev, row_width)  13.3 us
    another operation x1, local copies, waits for them, and re-layouts, shards(): buckets = local_grad.reshape(bucket_count, bucket_rows, row_width)  12.8 us
    another operation x1, local copies, waits for them, and re-layouts, shards(): slot_rows = gathered.reshape(bucket_count, bucket_rows, row_width)  12.8 us
  transfers between devices with their start and end apart: 1, of which 1 were waited for; matrix products, arithmetic and copies ran while one was open for 0% of the time, Pallas kernels for 0%

profile of v1, /device:TPU:32, one launch (start us, length us, event | category | flops | bytes accessed | tf_op | source)
XLA Modules:
  0.0 360.8 jit_solution(17003695365557141021)
XLA Ops:
  0.6 0.7 compare_and_fusion
  1.3 0.7 compare_select_fusion
  2.0 0.1 broadcast_in_dim.26
  2.1 0.1 copy.11
  2.2 0.1 copy.12
  2.3 12.8 %reshape_squeeze.3 = bf16[256,2,6144]{2,1,0:T(2,128)(2,1)} reshape(bf16[1,512,6144]{2,1,0:T(8,128)(2,1)} %param.7) | data formatting | bytes 12582912 | tf_op jit(solution)/shard_map/reshape;squeeze | solution.py:24
  15.2 21.4 %gather_fusion = bf16[256,2,6144]{2,1,0:T(2,128)(2,1)} fusion(bf16[256,2,6144]{2,1,0:T(2,128)(2,1)} %reshape_squeeze.3, s32[1024]{0:T(1024)S(1)} %pad_clamp_fusion), kind=kCustom, calls=%fused_computation | custom fusion | bytes 12583936 | tf_op jit(solution)/shard_map/jit(_take)/gather | solution.py:25
  36.6 13.3 %gather.7 = bf16[32,16,6144]{2,1,0:T(8,128)(2,1)} reshape(bf16[256,2,6144]{2,1,0:T(2,128)(2,1)} %gather_fusion) | data formatting | bytes 12582912 | tf_op jit(solution)/shard_map/jit(_take)/gather | solution.py:25
  49.9 3.4 broadcast_select_fusion
  53.3 79.7 %all_to_all.10 = bf16[32,16,6144]{2,1,0:T(8,128)(2,1)S(1)} all-to-all(bf16[32,16,6144]{2,1,0:T(8,128)(2,1)S(1)} %broadcast_select_fusion), channel_id=1, replica_groups=mesh['dp_0'=4,'dp_1'=4,'dp_2'=2,'expert'=4] {'dp_0','dp_1','dp_2'}, dimensions={0} | all-to-all | bytes 12582912 | tf_op jit(solution)/shard_map/all_to_all | solution.py:27
  133.0 0.0 copy-start.3
  133.0 0.0 copy-start
  133.0 0.0 copy-start.1
  133.0 0.0 copy-start.2
  133.1 1.0 convert_reduce_fusion
  134.1 0.7 multiply_reduce_fusion
  134.8 9.3 %psum.28 = f32[]{:T(128)} all-reduce(f32[]{:T(128)} %multiply_reduce_fusion), channel_id=1, replica_groups=mesh['dp_0'=4,'dp_1'=4,'dp_2'=2,'expert'=4] {'dp_0'}, use_global_device_ids=true, to_apply=%region_2.3 | all-reduce | flops 1 | bytes 8 | tf_op jit(solution)/shard_map/psum | solution.py:13
  144.0 10.4 %psum.29 = f32[]{:T(128)} all-reduce(f32[]{:T(128)} %psum.28), channel_id=1, replica_groups=mesh['dp_0'=4,'dp_1'=4,'dp_2'=2,'expert'=4] {'dp_1'}, use_global_device_ids=true, to_apply=%region_3.4 | all-reduce | flops 1 | bytes 8 | tf_op jit(solution)/shard_map/psum | solution.py:13
  154.5 0.0 copy-done.3
  154.5 3.1 psum.30
  158.2 11.1 %psum.31 = f32[]{:T(128)} all-reduce(f32[]{:T(128)} %psum.30), channel_id=1, replica_groups=mesh['dp_0'=4,'dp_1'=4,'dp_2'=2,'expert'=4] {'expert'}, use_global_device_ids=true, to_apply=%region_5.6 | all-reduce | flops 1 | bytes 8 | tf_op jit(solution)/shard_map/psum | solution.py:13
  170.1 0.0 copy-done
  170.1 0.0 copy-done.1
  170.1 0.0 copy-done.2
  170.1 0.4 fusion.9
  170.5 3.5 stack.2
  173.9 5.7 %all-to-all-start.1 = ((bf16[32,16,6144]{2,1,0:T(8,128)(2,1)}), bf16[32,16,6144]{2,1,0:T(8,128)(2,1)}, u32[]{:S(2)}, u32[]{:S(2)}) async-start(bf16[32,16,6144]{2,1,0:T(8,128)(2,1)} %stack.2), calls=%async_computation.1 | async-start | bytes 12582912 | tf_op jit(solution)/shard_map/all_to_all | solution.py:43
  179.6 1.2 multiply_subtract_fusion
  180.8 86.5 %all-to-all-done.1 = bf16[32,16,6144]{2,1,0:T(8,128)(2,1)} async-done(((bf16[32,16,6144]{2,1,0:T(8,128)(2,1)}), bf16[32,16,6144]{2,1,0:T(8,128)(2,1)}, u32[]{:S(2)}, u32[]{:S(2)}) %all-to-all-start.1) | async-done | bytes 6291488 | tf_op jit(solution)/shard_map/all_to_all | solution.py:43
  267.2 12.8 %reshape.121 = bf16[256,2,6144]{2,1,0:T(2,128)(2,1)} reshape(bf16[32,16,6144]{2,1,0:T(8,128)(2,1)} %all-to-all-done.1) | data formatting | bytes 12582912 | tf_op jit(solution)/shard_map/reshape;reshape | solution.py:45
  280.1 5.9 %broadcast_in_dim.32 = bf16[256,2,6144]{2,1,0:T(2,128)(2,1)} broadcast(bf16[]{:T(256)} %constant.13.clone.1), dimensions={} | broadcast | bytes 6291458 | tf_op jit(solution)/shard_map/broadcast_in_dim | solution.py:46
  286.0 61.5 %scatter_fusion = bf16[256,2,6144]{2,1,0:T(2,128)(2,1)} fusion(bf16[256,2,6144]{2,1,0:T(2,128)(2,1)} %broadcast_in_dim.32, s32[256]{0:T(256)S(1)} %compare_select_fusion, bf16[256,2,6144]{2,1,0:T(2,128)(2,1)} %reshape.121), kind=kCustom, calls=%fused_computation.1 | custom fusion | bytes 18875392 | tf_op jit(solution)/shard_map/scatter | solution.py:46
  347.5 13.3 %reshape.108 = bf16[512,6144]{1,0:T(8,128)(2,1)} reshape(bf16[256,2,6144]{2,1,0:T(2,128)(2,1)} %scatter_fusion) | data formatting | bytes 12582912 | tf_op jit(solution)/shard_map/reshape | solution.py:51
  (4 shorter events, 0.0 us)
Async XLA Ops:
  133.0 21.4 %copy-start.3 = (s32[1,1,16]{2,1,0:T(1,128)S(1)}, s32[1,1,16]{2,1,0:T(1,128)}, u32[]{:S(2)}) copy-start(s32[1,1,16]{2,1,0:T(1,128)} %param.12) | copy-start | bytes 196
  133.0 37.0 %copy-start = (f32[1,1,16,6144]{3,2,1,0:T(8,128)S(1)}, f32[1,1,16,6144]{3,2,1,0:T(8,128)}, u32[]{:S(2)}) copy-start(f32[1,1,16,6144]{3,2,1,0:T(8,128)} %param.9) | copy-start | bytes 1179652
  133.0 37.0 %copy-start.1 = (f32[1,1,16,6144]{3,2,1,0:T(8,128)S(1)}, f32[1,1,16,6144]{3,2,1,0:T(8,128)}, u32[]{:S(2)}) copy-start(f32[1,1,16,6144]{3,2,1,0:T(8,128)} %param.11) | copy-start | bytes 1179652
  133.0 37.0 %copy-start.2 = (f32[1,1,16,6144]{3,2,1,0:T(8,128)S(1)}, f32[1,1,16,6144]{3,2,1,0:T(8,128)}, u32[]{:S(2)}) copy-start(f32[1,1,16,6144]{3,2,1,0:T(8,128)} %param.10) | copy-start | bytes 1179652
  173.9 93.3 %all-to-all-start.1 = ((bf16[32,16,6144]{2,1,0:T(8,128)(2,1)}), bf16[32,16,6144]{2,1,0:T(8,128)(2,1)}, u32[]{:S(2)}, u32[]{:S(2)}) async-start(bf16[32,16,6144]{2,1,0:T(8,128)(2,1)} %stack.2), calls=%async_computation.1 | async-start | bytes 12582912 | tf_op jit(solution)/shard_map/all_to_all | solution.py:43
